TPU v7x, 256 devices: a whole 4x4x8 slice. The times are simulated.
256 devices in a mesh: dp: 8 (over x, y_hi), row: 32 (over y_lo, z, core).
Axes of the slice: x: 4, y: 4 (y_hi: 2, y_lo: 2; y = y_hi * 2 + y_lo), z: 8, core: 2. Of those that a mesh axis runs over, the one named last changes fastest.
Arguments:
- patch_queries: bfloat16 [8, 4096, 512], P('dp', 'row'), may hold values from -6 to 6
- patch_keys: bfloat16 [8, 4096, 512], P('dp', 'row'), may hold values from -6 to 6
- scan_input: float32 [8, 4096, 512], P('dp', 'row'), may hold values from -6 to 6
- decay_rate: float32 [8, 4096, 512], P('dp', 'row'), may hold values from 0.4 to 1, as said below
- gate_logit: bfloat16 [8, 4096, 512], P('dp', 'row'), may hold values from -6 to 6
- grad_output: bfloat16 [8, 4096, 1024], P('dp', 'row'), may hold values from -6 to 6
- output_weight: bfloat16 [1024, 512], replicated, may hold values from -0.25 to 0.25
Outputs:
- grad_queries: bfloat16 [8, 4096, 512], P('dp', 'row')
- grad_keys: bfloat16 [8, 4096, 512], P('dp', 'row')
- grad_input: float32 [8, 4096, 512], P('dp', 'row')
- grad_decay: float32 [8, 4096, 512], P('dp', 'row')
- grad_gate: bfloat16 [8, 4096, 512], P('dp', 'row')
- grad_weight: float32 [1024, 512], P(('dp', 'row'))
Inputs may be any that keep to these rules, and one draw needn't show every extreme that they name: `decay_rate`: forget gates lie strictly below 1.
All inputs are finite; a program needn't handle non-finite values.
Results may differ from a plain program's by a relative error of at most 0.012.
The roundings to bfloat16 on the way count: a program that leaves them out, or rounds other values in their place, can miss the bound.
Values may be sent and summed in bfloat16 or wider, within the bound.
No kernel may reach another device: no remote copies, remote signals or barrier semaphores. Data moves between devices by JAX's collectives and lax.ppermute only.
A program may use at most 128 MiB of HBM per device.

v0:
```python
import jax
import jax.numpy as jnp
from jax import lax
from jax.sharding import PartitionSpec as P

HEADS = 8
HEAD_DIM = 64
lowest_start = -1e30


def prefix(x, axis, combine, identity, reverse):
    length, index = (lax.axis_size(axis), lax.axis_index(axis))
    everything = jax.tree.map(lambda part: lax.all_gather(part, axis), x)
    start = jax.tree.map(
        lambda part, zero: jnp.broadcast_to(jnp.asarray(zero, part.dtype), part.shape), x, identity
    )

    def hop(k, before):
        at = length - 1 - k if reverse else k
        reached = at > index if reverse else at < index
        new = combine(before, jax.tree.map(lambda part: part[at], everything))
        return jax.tree.map(lambda a, b: jnp.where(reached, a, b), new, before)

    return lax.fori_loop(0, length, hop, start)


def compose(earlier, later):
    return (later[0] * earlier[0], later[0] * earlier[1] + later[1])


def silu_slope(gate_float):
    sigmoid_value = jax.nn.sigmoid(gate_float)
    return sigmoid_value * (1.0 + gate_float * (1.0 - sigmoid_value))


def block_layout(length):
    block_rows = 512
    return (block_rows, length // block_rows)


def to_heads(array):
    return array.reshape(array.shape[0], array.shape[1], HEADS, HEAD_DIM)


def carry_states(totals):
    return prefix(
        totals, "row", compose, (jnp.ones_like(totals[0]), jnp.zeros_like(totals[1])), False
    )[1]


def carry_adjoints(totals):
    return prefix(
        totals, "row", compose, (jnp.ones_like(totals[0]), jnp.zeros_like(totals[1])), True
    )[1]


def body(patch_queries, patch_keys, scan_input, decay_rate, gate_logit, grad_output, output_weight):
    scaling = HEAD_DIM ** (-0.5)
    image_count, row_count, channels = patch_queries.shape
    local_gain, local_states = lax.associative_scan(compose, (decay_rate, scan_input), axis=1)
    incoming = carry_states((local_gain[:, -1], local_states[:, -1]))
    states = local_states + local_gain * incoming[:, None]
    gate_float = gate_logit.astype(jnp.float32)
    activation = jax.nn.silu(gate_float)
    value_low = (states * activation).astype(jnp.bfloat16)
    grad_attended = jnp.einsum(
        "btd,dc->btc", grad_output, output_weight, preferred_element_type=jnp.float32
    ).astype(jnp.bfloat16)
    query_heads = to_heads(patch_queries)
    grad_heads = to_heads(grad_attended)
    key_heads = to_heads(patch_keys)
    value_heads = to_heads(value_low)
    start_top = jnp.full((image_count, HEADS, row_count), lowest_start, jnp.float32)
    zero_totals = jnp.zeros((image_count, HEADS, row_count), jnp.float32)
    zero_heads = jnp.zeros((image_count, row_count, HEADS, HEAD_DIM), jnp.float32)
    portion = lax.all_gather(patch_keys, "row", axis=1, tiled=True)
    block_rows, count_blocks = block_layout(portion.shape[1])

    def softmax_one_block(block_index, running):
        key_block = to_heads(
            lax.dynamic_slice_in_dim(portion, block_index * block_rows, block_rows, 1)
        )
        scores = (
            jnp.einsum(
                "bthd,bjhd->bhtj", query_heads, key_block, preferred_element_type=jnp.float32
            )
            * scaling
        )
        new_top = jnp.maximum(running[0], jnp.max(scores, axis=-1))
        new_sum = running[1] * jnp.exp(running[0] - new_top) + jnp.sum(
            jnp.exp(scores - new_top[..., None]), axis=-1
        )
        return (new_top, new_sum)

    running_top, total_sum = lax.fori_loop(
        0, count_blocks, softmax_one_block, (start_top, zero_totals)
    )
    log_total = running_top + jnp.log(total_sum)
    key_portion = lax.all_gather(patch_keys, "row", axis=1, tiled=True)
    value_portion = lax.all_gather(value_low, "row", axis=1, tiled=True)
    query_block_rows, count_blocks = block_layout(key_portion.shape[1])

    def query_one_block(block_index, running):
        attended_sum, row_delta, first_sum, second_sum = running
        key_block = to_heads(
            lax.dynamic_slice_in_dim(
                key_portion, block_index * query_block_rows, query_block_rows, 1
            )
        )
        value_block = to_heads(
            lax.dynamic_slice_in_dim(
                value_portion, block_index * query_block_rows, query_block_rows, 1
            )
        )
        scores = (
            jnp.einsum(
                "bthd,bjhd->bhtj", query_heads, key_block, preferred_element_type=jnp.float32
            )
            * scaling
        )
        weights = jnp.exp(scores - log_total[..., None])
        weights_low = weights.astype(jnp.bfloat16)
        grad_weights = jnp.einsum(
            "bthd,bjhd->bhtj", grad_heads, value_block, preferred_element_type=jnp.float32
        )
        row_delta = row_delta + jnp.sum(weights * grad_weights, axis=-1)
        weighted = (weights * grad_weights).astype(jnp.bfloat16)
        attended_sum = attended_sum + jnp.einsum(
            "bhtj,bjhd->bthd", weights_low, value_block, preferred_element_type=jnp.float32
        )
        first_sum = first_sum + jnp.einsum(
            "bhtj,bjhd->bthd", weighted, key_block, preferred_element_type=jnp.float32
        )
        second_sum = second_sum + jnp.einsum(
            "bhtj,bjhd->bthd", weights_low, key_block, preferred_element_type=jnp.float32
        )
        return (attended_sum, row_delta, first_sum, second_sum)

    folded = lax.fori_loop(
        0, count_blocks, query_one_block, (zero_heads, zero_totals, zero_heads, zero_heads)
    )
    attended_sum, row_delta, first_sum, second_sum = folded
    attended = attended_sum.astype(jnp.bfloat16).reshape(image_count, row_count, channels)
    delta_rows = jnp.transpose(row_delta, (0, 2, 1))[..., None]
    grad_queries = (
        ((first_sum - delta_rows * second_sum) * scaling)
        .astype(jnp.bfloat16)
        .reshape(image_count, row_count, channels)
    )
    all_totals, all_deltas = (
        lax.all_gather(jnp.transpose(log_total, (0, 2, 1)), "row", axis=1, tiled=True),
        lax.all_gather(jnp.transpose(row_delta, (0, 2, 1)), "row", axis=1, tiled=True),
    )
    query_portion = lax.all_gather(patch_queries, "row", axis=1, tiled=True)
    grad_portion = lax.all_gather(grad_attended, "row", axis=1, tiled=True)
    key_block_rows, count_blocks = block_layout(query_portion.shape[1])

    def key_one_block(block_index, running):
        key_sum, value_sum = running
        offset = block_index * key_block_rows
        query_block = to_heads(lax.dynamic_slice_in_dim(query_portion, offset, key_block_rows, 1))
        grad_block = to_heads(lax.dynamic_slice_in_dim(grad_portion, offset, key_block_rows, 1))
        total_block = jnp.transpose(
            lax.dynamic_slice_in_dim(all_totals, offset, key_block_rows, 1), (0, 2, 1)
        )
        delta_block = jnp.transpose(
            lax.dynamic_slice_in_dim(all_deltas, offset, key_block_rows, 1), (0, 2, 1)
        )
        scores = (
            jnp.einsum(
                "bthd,bjhd->bhtj", query_block, key_heads, preferred_element_type=jnp.float32
            )
            * scaling
        )
        weights = jnp.exp(scores - total_block[..., None])
        grad_weights = jnp.einsum(
            "bthd,bjhd->bhtj", grad_block, value_heads, preferred_element_type=jnp.float32
        )
        grad_scores = (weights * (grad_weights - delta_block[..., None])).astype(jnp.bfloat16)
        key_sum = key_sum + jnp.einsum(
            "bhtj,bthd->bjhd", grad_scores, query_block, preferred_element_type=jnp.float32
        )
        value_sum = value_sum + jnp.einsum(
            "bhtj,bthd->bjhd",
            weights.astype(jnp.bfloat16),
            grad_block,
            preferred_element_type=jnp.float32,
        )
        return (key_sum, value_sum)

    key_sum, value_sum = lax.fori_loop(0, count_blocks, key_one_block, (zero_heads, zero_heads))
    grad_keys = (key_sum * scaling).astype(jnp.bfloat16).reshape(image_count, row_count, channels)
    value_gradient = value_sum.reshape(image_count, row_count, channels)
    grad_gate = (value_gradient * states * silu_slope(gate_float)).astype(jnp.bfloat16)
    shifted = jnp.concatenate([decay_rate[:, 1:], jnp.ones_like(decay_rate[:, :1])], axis=1)
    tail_gain, local_adjoint = lax.associative_scan(
        compose, (shifted, value_gradient * activation), reverse=True, axis=1
    )
    head_rate = decay_rate[:, 0]
    arriving = carry_adjoints((head_rate * tail_gain[:, 0], head_rate * local_adjoint[:, 0]))
    grad_input = local_adjoint + tail_gain * arriving[:, None]
    earlier = jnp.concatenate([incoming[:, None], states[:, :-1]], axis=1)
    grad_decay = grad_input * earlier
    grad_weight = lax.psum_scatter(
        jnp.einsum("btd,btc->dc", grad_output, attended, preferred_element_type=jnp.float32),
        ("dp", "row"),
        scatter_dimension=0,
        tiled=True,
    )
    return (grad_queries, grad_keys, grad_input, grad_decay, grad_gate, grad_weight)


def solution(mesh):
    in_specs = (
        P("dp", "row", None),
        P("dp", "row", None),
        P("dp", "row", None),
        P("dp", "row", None),
        P("dp", "row", None),
        P("dp", "row", None),
        P(),
    )
    out_specs = (
        P("dp", "row", None),
        P("dp", "row", None),
        P("dp", "row", None),
        P("dp", "row", None),
        P("dp", "row", None),
        P(("dp", "row"), None),
    )
    return jax.shard_map(body, mesh=mesh, in_specs=in_specs, out_specs=out_specs, check_vma=False)
```

profile of v0, /device:TPU:2, one launch (start us, length us, event | category | flops | bytes accessed | tf_op | source)
XLA Modules:
  0.0 1026.0 jit_solution(15914821030163046469)
XLA Ops:
  13.7 3.7 slice.487
  20.7 3.7 slice.446
  153.4 4.8 pad.201
  167.0 4.3 pad.200
  171.6 4.6 pad.187
  176.5 4.3 pad.186
  181.1 37.3 %all_gather.33 = f32[32,1,512]{2,1,0:T(1,128)S(1)} all-gather(f32[1,1,512]{2,1,0:T(1,128)S(1)} %copy.196), channel_id=1, replica_groups=mesh['dp'=8,'row'=32] {'row'}, dimensions={0}, use_global_device_ids=true | all-gather | bytes 67584 | tf_op jit(solution)/shard_map/all_gather | solution.py:13
  218.5 30.8 %all_gather.34 = f32[32,1,512]{2,1,0:T(1,128)S(1)} all-gather(f32[1,1,512]{2,1,0:T(1,128)S(1)} %copy.197), channel_id=1, replica_groups=mesh['dp'=8,'row'=32] {'row'}, dimensions={0}, use_global_device_ids=true | all-gather | bytes 67584 | tf_op jit(solution)/shard_map/all_gather | solution.py:13
  255.4 6.0 slice.507
  261.5 6.0 slice.509
  267.5 6.4 slice.516
  279.5 16.3 %while.83 = (s32[]{:T(128)}, f32[1,8,128]{2,1,0:T(8,128)S(1)}, f32[1,8,128]{2,1,0:T(8,128)S(1)}, bf16[1,4096,512]{1,2,0:T(8,128)(2,1)}, bf16[1,128,8,64]{1,3,2,0...) while((s32[]{:T(128)}, f32[1,8,128]{2,1,0:T(8,128)S(1)}, ...), condition=%wide.region_5.6_spmd.clone, body=%wide.region_2.5_spmd.clone.sunk | while | flops 69735432 | bytes 5951650 | solution.py:95
  295.8 35.0 %all_gather.38 = f32[1,4096,8]{1,2,0:T(8,128)} all-gather(f32[1,128,8]{1,2,0:T(8,128)S(1)} %bitcast.269), channel_id=1, replica_groups=mesh['dp'=8,'row'=32] {'row'}, dimensions={1}, use_global_device_ids=true | all-gather | bytes 135168 | tf_op jit(solution)/shard_map/all_gather | solution.py:151
  330.9 56.9 %while.84 = (s32[]{:T(128)}, f32[1,128,8,64]{1,3,2,0:T(8,128)}, f32[1,8,128]{2,1,0:T(8,128)S(1)}, f32[1,128,8,64]{1,3,2,0:T(8,128)S(1)}, f32[1,128,8,64]{1,3,2,0...) while((s32[]{:T(128)}, f32[1,128,8,64]{1,3,2,0:T(8,128)}, ...), condition=%wide.region_8.9_spmd.clone, body=%wide.region_6.8_spmd.clone.sunk | while | flops 341705728 | bytes 17592552 | solution.py:139
  387.8 33.9 %all_gather.40 = f32[1,4096,8]{1,2,0:T(8,128)} all-gather(f32[1,128,8]{1,2,0:T(8,128)S(1)} %bitcast.277), channel_id=1, replica_groups=mesh['dp'=8,'row'=32] {'row'}, dimensions={1}, use_global_device_ids=true | all-gather | bytes 135168 | tf_op jit(solution)/shard_map/all_gather | solution.py:152
  421.6 40.4 %all-gather.12.cloned.1.call-done = bf16[4096,512]{1,0:T(8,128)(2,1)} async-done(((bf16[128,512]{1,0:T(8,128)(2,1)}), bf16[4096,512]{1,0:T(8,128)(2,1)}) %all-gather.12.cloned.1.call-update) | async-done | bytes 4194320 | tf_op jit(solution)/shard_map/all_gather | solution.py:155
  462.0 85.3 %while.85 = (s32[]{:T(128)}, f32[1,128,8,64]{1,3,2,0:T(8,128)}, f32[1,128,8,64]{1,3,2,0:T(8,128)}, bf16[1,4096,512]{1,2,0:T(8,128)(2,1)}, bf16[1,128,8,64]{1,3,2...) while((s32[]{:T(128)}, f32[1,128,8,64]{1,3,2,0:T(8,128)}, ...), condition=%wide.region_10.11_spmd.clone, body=%wide.region_9.10_spmd.clone.sunk | while | flops 272891904 | bytes 15057126 | solution.py:191
  476.7 3.5 fusion.117
  509.0 3.5 fusion.117
  519.7 3.5 fusion.117
  548.6 6.0 slice.513
  554.6 6.4 slice.511
  618.3 3.7 slice.518
  622.0 3.7 slice.559
  625.7 6.7 slice.561
  672.7 4.3 pad.214
  677.0 4.4 pad.215
  681.6 4.6 pad.228
  686.2 4.4 pad.229
  691.0 32.0 %all_gather.41 = f32[32,1,512]{2,1,0:T(1,128)S(1)} all-gather(f32[1,1,512]{2,1,0:T(1,128)S(1)} %copy.218), channel_id=1, replica_groups=mesh['dp'=8,'row'=32] {'row'}, dimensions={0}, use_global_device_ids=true | all-gather | bytes 67584 | tf_op jit(solution)/shard_map/all_gather | solution.py:13
  723.1 31.0 %all_gather.42 = f32[32,1,512]{2,1,0:T(1,128)S(1)} all-gather(f32[1,1,512]{2,1,0:T(1,128)S(1)} %copy.219), channel_id=1, replica_groups=mesh['dp'=8,'row'=32] {'row'}, dimensions={0}, use_global_device_ids=true | all-gather | bytes 67584 | tf_op jit(solution)/shard_map/all_gather | solution.py:13
  763.6 253.6 %all-reduce.61.cloned.1.call-done = f32[1024,512]{0,1:T(8,128)} async-done(((f32[1024,512]{0,1:T(8,128)}), f32[1024,512]{0,1:T(8,128)}) %all-reduce.61.cloned.1.call-update) | async-done | bytes 2097168
  (600 shorter events, 417.4 us)
Async XLA Ops:
  7.2 245.3 %copy-start = (bf16[1024,512]{1,0:T(8,128)(2,1)S(1)}, bf16[1024,512]{1,0:T(8,128)(2,1)}, u32[]{:S(2)}) copy-start(bf16[1024,512]{1,0:T(8,128)(2,1)} %param.23) | copy-start | bytes 3145732
  7.2 272.3 %all-gather.8.cloned.1.call-start = ((), (), s32[]{:S(2)}) async-start(), calls=%async_computation.1 | async-start | bytes 4325376 | tf_op jit(solution)/shard_map/all_gather | solution.py:99
  9.0 321.9 %all-gather.6.cloned.1.call-start = ((), (), s32[]{:S(2)}) async-start(), calls=%async_computation | async-start | bytes 4325376 | tf_op jit(solution)/shard_map/all_gather | solution.py:100
  72.9 12.6 %copy-start.12 = (f32[1,128,512]{2,1,0:T(8,128)S(1)}, f32[1,128,512]{2,1,0:T(8,128)}, u32[]{:S(2)}) copy-start(f32[1,128,512]{2,1,0:T(8,128)} %param.20) | copy-start | bytes 786436
  89.2 161.4 %copy-start.14 = (bf16[1,128,512]{1,2,0:T(8,128)(2,1)}, bf16[1,128,512]{1,2,0:T(8,128)(2,1)S(1)}, u32[]{:S(2)}) copy-start(bf16[1,128,512]{1,2,0:T(8,128)(2,1)S(1)} %copy.198) | copy-start | bytes 393220
  121.2 5.2 copy-start.8
  141.6 5.5 copy-start.29
  148.8 14.4 %copy-start.27 = (f32[1,31,512]{1,2,0:T(8,128)S(1)}, f32[1,31,512]{1,2,0:T(8,128)}, u32[]{:S(2)}) copy-start(f32[1,31,512]{1,2,0:T(8,128)} %get-tuple-element.1003) | copy-start | bytes 190468
  153.3 12.2 %copy-start.35 = (f32[1,1,512]{2,1,0:T(1,128)S(1)}, f32[1,1,512]{2,1,0:T(1,128)}, u32[]{:S(2)}) copy-start(f32[1,1,512]{2,1,0:T(1,128)} %slice.490) | copy-start | bytes 6148
  165.7 5.6 copy-start.9
  165.7 10.5 %copy-start.34 = (f32[1,1,512]{2,1,0:T(1,128)S(1)}, f32[1,1,512]{2,1,0:T(1,128)}, u32[]{:S(2)}) copy-start(f32[1,1,512]{2,1,0:T(1,128)} %slice.439) | copy-start | bytes 6148
  176.3 75.3 %copy-start.32 = (bf16[1,128,512]{2,1,0:T(8,128)(2,1)S(1)}, bf16[1,128,512]{2,1,0:T(8,128)(2,1)}, u32[]{:S(2)}) copy-start(bf16[1,128,512]{2,1,0:T(8,128)(2,1)} %param.17) | copy-start | bytes 393220
  176.5 76.0 %copy-start.20 = (bf16[1,128,1024]{2,1,0:T(8,128)(2,1)S(1)}, bf16[1,128,1024]{2,1,0:T(8,128)(2,1)}, u32[]{:S(2)}) copy-start(bf16[1,128,1024]{2,1,0:T(8,128)(2,1)} %param.22) | copy-start | bytes 786436
  249.3 5.9 copy-start.13
  251.6 170.1 %all-gather.10.cloned.1.call-start = ((), (), s32[]{:S(2)}) async-start(), calls=%async_computation.2 | async-start | bytes 4325376 | tf_op jit(solution)/shard_map/all_gather | solution.py:154
  252.4 209.6 %all-gather.12.cloned.1.call-start = ((), (), s32[]{:S(2)}) async-start(), calls=%async_computation.3 | async-start | bytes 4325376 | tf_op jit(solution)/shard_map/all_gather | solution.py:155
  253.5 763.7 %all-reduce.61.cloned.1.call-start = ((), (), s32[]{:S(2)}) async-start(), calls=%async_computation.4 | async-start | bytes 4194304
  255.4 24.1 %copy-start.3 = (bf16[1,128,512]{1,2,0:T(8,128)(2,1)S(1)}, bf16[1,128,512]{1,2,0:T(8,128)(2,1)}, u32[]{:S(2)}) copy-start(bf16[1,128,512]{1,2,0:T(8,128)(2,1)} %copy.200) | copy-start | bytes 393220
  547.3 14.5 %copy-start.25 = (f32[1,64,512]{1,2,0:T(8,128)S(1)}, f32[1,64,512]{1,2,0:T(8,128)}, u32[]{:S(2)}) copy-start(f32[1,64,512]{1,2,0:T(8,128)} %slice.510) | copy-start | bytes 393220
  547.3 14.5 %copy-start.26 = (f32[1,64,512]{1,2,0:T(8,128)S(1)}, f32[1,64,512]{1,2,0:T(8,128)}, u32[]{:S(2)}) copy-start(f32[1,64,512]{1,2,0:T(8,128)} %slice.517) | copy-start | bytes 393220
  610.6 22.6 %copy-start.17 = (f32[1,2,512]{1,2,0:T(8,128)S(1)}, f32[1,2,512]{1,2,0:T(8,128)}, u32[]{:S(2)}) copy-start(f32[1,2,512]{1,2,0:T(8,128)} %pad_add_fusion) | copy-start | bytes 12292
  612.5 21.0 %copy-start.15 = (f32[1,1,512]{1,2,0:T(8,128)S(1)}, f32[1,1,512]{1,2,0:T(8,128)}, u32[]{:S(2)}) copy-start(f32[1,1,512]{1,2,0:T(8,128)} %get-tuple-element.980) | copy-start | bytes 6148
  612.5 21.0 %copy-start.16 = (f32[1,1,512]{1,2,0:T(8,128)S(1)}, f32[1,1,512]{1,2,0:T(8,128)}, u32[]{:S(2)}) copy-start(f32[1,1,512]{1,2,0:T(8,128)} %get-tuple-element.981) | copy-start | bytes 6148
  659.1 4.7 copy-start.30
  663.8 3.6 copy-start.22
  667.4 5.0 copy-start.28
  672.5 18.0 %copy-start.10 = (f32[1,1,512]{1,2,0:T(8,128)S(1)}, f32[1,1,512]{1,2,0:T(8,128)}, u32[]{:S(2)}) copy-start(f32[1,1,512]{1,2,0:T(8,128)} %copy-done.9) | copy-start | bytes 6148
  681.4 72.7 %copy-start.4 = (f32[1,128,8,64]{1,3,2,0:T(8,128)S(1)}, f32[1,128,8,64]{1,3,2,0:T(8,128)}, u32[]{:S(2)}) copy-start(f32[1,128,8,64]{1,3,2,0:T(8,128)} %get-tuple-element.663) | copy-start | bytes 786436
  681.6 72.6 %copy-start.21 = (bf16[1,128,1024]{2,1,0:T(8,128)(2,1)S(1)}, bf16[1,128,1024]{2,1,0:T(8,128)(2,1)}, u32[]{:S(2)}) copy-start(bf16[1,128,1024]{2,1,0:T(8,128)(2,1)} %param.22) | copy-start | bytes 786436
  756.0 3.5 copy-start.31
  757.5 3.4 copy-start.11
  760.2 258.8 %copy-start.1 = (bf16[1024,512]{1,0:T(8,128)(2,1)S(1)}, bf16[1024,512]{1,0:T(8,128)(2,1)}, u32[]{:S(2)}) copy-start(bf16[1024,512]{1,0:T(8,128)(2,1)} %param.23) | copy-start | bytes 3145732
  (23 other events, 47.2 us)
Sparse Core Ops, SparseCore 0:
  10.3 75.1 all-gather.7
  251.7 69.4 all-gather.5
  323.6 71.0 all-gather.9
  396.4 65.5 all-gather.11
  756.1 261.0 all-reduce.60
where the time goes:
time: 1040 us; the launch traced here: 1030 us
  local copies, waits for them, and re-layouts  344 us (33%)
  waiting for transfers between devices  294 us (28%)
  blocking collectives  200 us (19%)
  matrix products  113 us (11%)
  other arithmetic  56 us (5%)
  between operations  15.7 us (2%)
    unnamed x6, waiting for transfers between devices  254 us
    all_gather x4, blocking collectives, prefix(): everything = jax.tree.map(lambda part: lax.all_gather(part, axis), x)  131 us
    slice x42, local copies, waits for them, and re-layouts, body(): lax.associative_scan(compose, (shifted, value_gradient * activation), rev...  101 us
    slice x37, local copies, waits for them, and re-layouts, body(): lax.associative_scan(compose, (decay_rate, scan_input), axis=1)  70.4 us
    pad x24, local copies, waits for them, and re-layouts, body(): lax.associative_scan(compose, (decay_rate, scan_input), axis=1)  54.1 us
    all_gather x1, waiting for transfers between devices, body(): grad_portion = lax.all_gather(grad_attended, 'row', axis=1, tiled=True)  40.4 us
    pad x24, local copies, waits for them, and re-layouts, body(): lax.associative_scan(compose, (shifted, value_gradient * activation), rev...  39.2 us
    all_gather x1, blocking collectives, body(): lax.all_gather(jnp.transpose(log_total, (0, 2, 1)), 'row', axis=1, tiled=...  35 us
  transfers between devices with their start and end apart: 5, of which 2 were waited for; matrix products, arithmetic and copies ran while one was open for 27% of the time, Pallas kernels for 0%

commit v1 on v0

--- a/solution.py
+++ b/solution.py
@@ -148,7 +148,12 @@
         .reshape(image_count, row_count, channels)
     )
     all_totals, all_deltas = (
-        lax.all_gather(jnp.transpose(log_total, (0, 2, 1)), "row", axis=1, tiled=True),
+        jnp.concatenate(
+            lax.all_to_all(
+                jnp.stack([jnp.transpose(log_total, (0, 2, 1))] * lax.axis_size("row")), "row", 0, 0
+            ),
+            axis=1,
+        ),
         lax.all_gather(jnp.transpose(row_delta, (0, 2, 1)), "row", axis=1, tiled=True),
     )
     query_portion = lax.all_gather(patch_queries, "row", axis=1, tiled=True)

time: 1040 us -> 759 us (0.73)
  waiting for transfers between devices: 294 us -> 61.1 us
  blocking collectives: 200 us -> 169 us
  matrix products: 113 us -> 97.4 us
    unnamed x6, waiting for transfers between devices: 254 us -> 0.08 us
    all_gather x1 -> x0, blocking collectives: 35 us -> none  [body(): lax.all_gather(jnp.transpose(log_total, (0, 2, 1)), 'row', axis=1, tiled=...]
    all_gather x1, waiting for transfers between devices: 0.01 us -> 25 us  [body(): value_portion = lax.all_gather(value_low, 'row', axis=1, tiled=True)]
    unnamed x98 -> x96, local copies, waits for them, and re-layouts: 21.7 us -> 21.7 us
  transfers between devices with their start and end apart: 5 -> 6, of which waited for: 2 -> 2; matrix products, arithmetic and copies ran while one was open for 27% -> 65% of each run, Pallas kernels for 0% -> 0%
where the time goes in v1:
time: 759 us; the launch traced here: 744 us
  local copies, waits for them, and re-layouts  340 us (45%)
  blocking collectives  169 us (22%)
  matrix products  97.4 us (13%)
  waiting for transfers between devices  61.1 us (8%)
  other arithmetic  52.5 us (7%)
  between operations  15.8 us (2%)
    all_gather x4, blocking collectives, prefix(): everything = jax.tree.map(lambda part: lax.all_gather(part, axis), x)  131 us
    slice x42, local copies, waits for them, and re-layouts, body(): lax.associative_scan(compose, (shifted, value_gradient * activation), rev...  98.7 us
    slice x37, local copies, waits for them, and re-layouts, body(): lax.associative_scan(compose, (decay_rate, scan_input), axis=1)  70.3 us
    pad x24, local copies, waits for them, and re-layouts, body(): lax.associative_scan(compose, (decay_rate, scan_input), axis=1)  54.1 us
    pad x24, local copies, waits for them, and re-layouts, body(): lax.associative_scan(compose, (shifted, value_gradient * activation), rev...  37.3 us
    all_gather x1, blocking collectives, body(): lax.all_gather(jnp.transpose(row_delta, (0, 2, 1)), 'row', axis=1, tiled=...  37.2 us
    all_gather x1, waiting for transfers between devices, body(): grad_portion = lax.all_gather(grad_attended, 'row', axis=1, tiled=True)  36 us
    dot_general x8, matrix products, key_one_block(): jnp.einsum('bhtj,bthd->bjhd', grad_scores, query_block, preferred_element...  27.8 us
  transfers between devices with their start and end apart: 6, of which 2 were waited for; matrix products, arithmetic and copies ran while one was open for 65% of the time, Pallas kernels for 0%

profile of v1, /device:TPU:2, one launch (start us, length us, event | category | flops | bytes accessed | tf_op | source)
XLA Modules:
  0.0 744.4 jit_solution(4293749214183398418)
XLA Ops:
  13.7 3.7 slice.487
  20.7 3.7 slice.446
  153.3 4.8 pad.201
  166.9 4.3 pad.200
  171.6 4.6 pad.187
  176.4 4.3 pad.186
  181.1 37.4 %all_gather.30 = f32[32,1,512]{2,1,0:T(1,128)S(1)} all-gather(f32[1,1,512]{2,1,0:T(1,128)S(1)} %copy.196), channel_id=1, replica_groups=mesh['dp'=8,'row'=32] {'row'}, dimensions={0}, use_global_device_ids=true | all-gather | bytes 67584 | tf_op jit(solution)/shard_map/all_gather | solution.py:13
  218.5 30.8 %all_gather.31 = f32[32,1,512]{2,1,0:T(1,128)S(1)} all-gather(f32[1,1,512]{2,1,0:T(1,128)S(1)} %copy.197), channel_id=1, replica_groups=mesh['dp'=8,'row'=32] {'row'}, dimensions={0}, use_global_device_ids=true | all-gather | bytes 67584 | tf_op jit(solution)/shard_map/all_gather | solution.py:13
  255.4 6.0 slice.507
  261.4 6.0 slice.509
  267.5 6.4 slice.516
  279.3 16.3 %while.83 = (s32[]{:T(128)}, f32[1,8,128]{2,1,0:T(8,128)S(1)}, f32[1,8,128]{2,1,0:T(8,128)S(1)}, bf16[1,4096,512]{1,2,0:T(8,128)(2,1)}, bf16[1,128,8,64]{1,3,2,0...) while((s32[]{:T(128)}, f32[1,8,128]{2,1,0:T(8,128)S(1)}, ...), condition=%wide.region_5.6_spmd.clone, body=%wide.region_2.5_spmd.clone.sunk | while | flops 69735432 | bytes 5951650 | solution.py:95
  295.6 25.0 %all-gather.6.cloned.1.call-done = bf16[1,4096,512]{1,2,0:T(8,128)(2,1)} async-done(((bf16[1,128,512]{1,2,0:T(8,128)(2,1)}), bf16[1,4096,512]{1,2,0:T(8,128)(2,1)}) %all-gather.6.cloned.1.call-update) | async-done | bytes 4194320 | tf_op jit(solution)/shard_map/all_gather | solution.py:100
  320.7 56.9 %while.84 = (s32[]{:T(128)}, f32[1,128,8,64]{1,3,2,0:T(8,128)}, f32[1,8,128]{2,1,0:T(8,128)S(1)}, f32[1,128,8,64]{1,3,2,0:T(8,128)S(1)}, f32[1,128,8,64]{1,3,2,0...) while((s32[]{:T(128)}, f32[1,128,8,64]{1,3,2,0:T(8,128)}, ...), condition=%wide.region_8.9_spmd.clone, body=%wide.region_6.8_spmd.clone.sunk | while | flops 341705728 | bytes 17592552 | solution.py:139
  380.0 5.9 all-to-all-start
  389.8 37.2 %all_gather.36 = f32[1,4096,8]{1,2,0:T(8,128)} all-gather(f32[1,128,8]{1,2,0:T(8,128)S(1)} %bitcast.281), channel_id=1, replica_groups=mesh['dp'=8,'row'=32] {'row'}, dimensions={1}, use_global_device_ids=true | all-gather | bytes 135168 | tf_op jit(solution)/shard_map/all_gather | solution.py:157
  427.0 36.0 %all-gather.12.cloned.1.call-done = bf16[4096,512]{1,0:T(8,128)(2,1)} async-done(((bf16[128,512]{1,0:T(8,128)(2,1)}), bf16[4096,512]{1,0:T(8,128)(2,1)}) %all-gather.12.cloned.1.call-update) | async-done | bytes 4194320 | tf_op jit(solution)/shard_map/all_gather | solution.py:160
  463.0 71.2 %while.85 = (s32[]{:T(128)}, f32[1,128,8,64]{1,3,2,0:T(8,128)}, f32[1,128,8,64]{1,3,2,0:T(8,128)S(1)}, bf16[1,4096,512]{1,2,0:T(8,128)(2,1)}, bf16[1,128,8,64]{1...) while((s32[]{:T(128)}, f32[1,128,8,64]{1,3,2,0:T(8,128)}, ...), condition=%wide.region_10.11_spmd.clone, body=%wide.region_9.10_spmd.clone.sunk | while | flops 272891904 | bytes 15057126 | solution.py:196
  484.9 3.5 fusion.117
  493.8 3.5 fusion.117
  502.7 3.5 fusion.117
  535.5 6.0 slice.513
  541.5 6.4 slice.511
  601.3 3.7 slice.518
  605.0 3.7 slice.559
  608.7 6.7 slice.561
  648.1 4.3 pad.214
  652.5 4.4 pad.215
  657.0 4.6 pad.228
  661.6 4.4 pad.229
  666.4 32.4 %all_gather.37 = f32[32,1,512]{2,1,0:T(1,128)S(1)} all-gather(f32[1,1,512]{2,1,0:T(1,128)S(1)} %copy.218), channel_id=1, replica_groups=mesh['dp'=8,'row'=32] {'row'}, dimensions={0}, use_global_device_ids=true | all-gather | bytes 67584 | tf_op jit(solution)/shard_map/all_gather | solution.py:13
  699.0 30.9 %all_gather.38 = f32[32,1,512]{2,1,0:T(1,128)S(1)} all-gather(f32[1,1,512]{2,1,0:T(1,128)S(1)} %copy.219), channel_id=1, replica_groups=mesh['dp'=8,'row'=32] {'row'}, dimensions={0}, use_global_device_ids=true | all-gather | bytes 67584 | tf_op jit(solution)/shard_map/all_gather | solution.py:13
  (600 shorter events, 394.0 us)
Async XLA Ops:
  7.2 245.3 %copy-start = (bf16[1024,512]{1,0:T(8,128)(2,1)S(1)}, bf16[1024,512]{1,0:T(8,128)(2,1)}, u32[]{:S(2)}) copy-start(bf16[1024,512]{1,0:T(8,128)(2,1)} %param.23) | copy-start | bytes 3145732
  7.2 272.2 %all-gather.8.cloned.1.call-start = ((), (), s32[]{:S(2)}) async-start(), calls=%async_computation.2 | async-start | bytes 4325376 | tf_op jit(solution)/shard_map/all_gather | solution.py:99
  9.0 311.7 %all-gather.6.cloned.1.call-start = ((), (), s32[]{:S(2)}) async-start(), calls=%async_computation.1 | async-start | bytes 4325376 | tf_op jit(solution)/shard_map/all_gather | solution.py:100
  72.9 12.6 %copy-start.13 = (f32[1,128,512]{2,1,0:T(8,128)S(1)}, f32[1,128,512]{2,1,0:T(8,128)}, u32[]{:S(2)}) copy-start(f32[1,128,512]{2,1,0:T(8,128)} %param.20) | copy-start | bytes 786436
  89.1 161.5 %copy-start.15 = (bf16[1,128,512]{1,2,0:T(8,128)(2,1)}, bf16[1,128,512]{1,2,0:T(8,128)(2,1)S(1)}, u32[]{:S(2)}) copy-start(bf16[1,128,512]{1,2,0:T(8,128)(2,1)S(1)} %copy.198) | copy-start | bytes 393220
  121.1 5.2 copy-start.9
  141.5 5.5 copy-start.27
  148.7 14.4 %copy-start.25 = (f32[1,31,512]{1,2,0:T(8,128)S(1)}, f32[1,31,512]{1,2,0:T(8,128)}, u32[]{:S(2)}) copy-start(f32[1,31,512]{1,2,0:T(8,128)} %get-tuple-element.1003) | copy-start | bytes 190468
  153.3 12.2 %copy-start.34 = (f32[1,1,512]{2,1,0:T(1,128)S(1)}, f32[1,1,512]{2,1,0:T(1,128)}, u32[]{:S(2)}) copy-start(f32[1,1,512]{2,1,0:T(1,128)} %slice.490) | copy-start | bytes 6148
  165.6 5.6 copy-start.10
  165.7 10.5 %copy-start.33 = (f32[1,1,512]{2,1,0:T(1,128)S(1)}, f32[1,1,512]{2,1,0:T(1,128)}, u32[]{:S(2)}) copy-start(f32[1,1,512]{2,1,0:T(1,128)} %slice.439) | copy-start | bytes 6148
  176.3 75.3 %copy-start.31 = (bf16[1,128,512]{2,1,0:T(8,128)(2,1)S(1)}, bf16[1,128,512]{2,1,0:T(8,128)(2,1)}, u32[]{:S(2)}) copy-start(bf16[1,128,512]{2,1,0:T(8,128)(2,1)} %param.17) | copy-start | bytes 393220
  176.4 76.0 %copy-start.19 = (bf16[1,128,1024]{2,1,0:T(8,128)(2,1)S(1)}, bf16[1,128,1024]{2,1,0:T(8,128)(2,1)}, u32[]{:S(2)}) copy-start(bf16[1,128,1024]{2,1,0:T(8,128)(2,1)} %param.22) | copy-start | bytes 786436
  249.3 5.9 copy-start.14
  251.5 175.5 %all-gather.10.cloned.1.call-start = ((), (), s32[]{:S(2)}) async-start(), calls=%async_computation.3 | async-start | bytes 4325376 | tf_op jit(solution)/shard_map/all_gather | solution.py:159
  252.4 210.7 %all-gather.12.cloned.1.call-start = ((), (), s32[]{:S(2)}) async-start(), calls=%async_computation.4 | async-start | bytes 4325376 | tf_op jit(solution)/shard_map/all_gather | solution.py:160
  255.3 24.0 %copy-start.3 = (bf16[1,128,512]{1,2,0:T(8,128)(2,1)S(1)}, bf16[1,128,512]{1,2,0:T(8,128)(2,1)}, u32[]{:S(2)}) copy-start(bf16[1,128,512]{1,2,0:T(8,128)(2,1)} %copy.200) | copy-start | bytes 393220
  380.0 83.0 %all-to-all-start = ((f32[32,1,128,8]{2,3,1,0:T(8,128)}), f32[32,1,128,8]{2,3,1,0:T(8,128)}, u32[]{:S(2)}, u32[]{:S(2)}) async-start(f32[32,1,128,8]{2,3,1,0:T(8,128)} %stack.2), calls=%async_computation | async-start | bytes 262144 | tf_op jit(solution)/shard_map/all_to_all | solution.py:152
  385.9 349.7 %all-reduce.61.cloned.1.call-start = ((), (), s32[]{:S(2)}) async-start(), calls=%async_computation.5 | async-start | bytes 4194304
  387.0 76.1 %copy-start.4 = (f32[1,128,8,64]{1,3,2,0:T(8,128)S(1)}, f32[1,128,8,64]{1,3,2,0:T(8,128)}, u32[]{:S(2)}) copy-start(f32[1,128,8,64]{1,3,2,0:T(8,128)} %custom-call.8) | copy-start | bytes 786436
  387.0 76.1 %copy-start.6 = (bf16[1,128,512]{1,2,0:T(8,128)(2,1)S(1)}, bf16[1,128,512]{1,2,0:T(8,128)(2,1)}, u32[]{:S(2)}) copy-start(bf16[1,128,512]{1,2,0:T(8,128)(2,1)} %copy.199) | copy-start | bytes 393220
  534.2 14.5 %copy-start.23 = (f32[1,64,512]{1,2,0:T(8,128)S(1)}, f32[1,64,512]{1,2,0:T(8,128)}, u32[]{:S(2)}) copy-start(f32[1,64,512]{1,2,0:T(8,128)} %slice.510) | copy-start | bytes 393220
  534.3 14.5 %copy-start.24 = (f32[1,64,512]{1,2,0:T(8,128)S(1)}, f32[1,64,512]{1,2,0:T(8,128)}, u32[]{:S(2)}) copy-start(f32[1,64,512]{1,2,0:T(8,128)} %slice.517) | copy-start | bytes 393220
  593.7 22.6 %copy-start.16 = (f32[1,2,512]{1,2,0:T(8,128)S(1)}, f32[1,2,512]{1,2,0:T(8,128)}, u32[]{:S(2)}) copy-start(f32[1,2,512]{1,2,0:T(8,128)} %pad_add_fusion) | copy-start | bytes 12292
  635.5 4.7 copy-start.28
  642.9 5.0 copy-start.26
  648.0 18.0 %copy-start.11 = (f32[1,1,512]{1,2,0:T(8,128)S(1)}, f32[1,1,512]{1,2,0:T(8,128)}, u32[]{:S(2)}) copy-start(f32[1,1,512]{1,2,0:T(8,128)} %copy-done.10) | copy-start | bytes 6148
  656.8 73.0 %copy-start.32 = (f32[1,512]{1,0:T(1,128)S(1)}, f32[1,512]{1,0:T(1,128)}, u32[]{:S(2)}) copy-start(f32[1,512]{1,0:T(1,128)} %custom-call.9) | copy-start | bytes 6148
  666.0 65.4 %copy-start.30 = (f32[1,128,8,64]{1,3,2,0:T(8,128)S(1)}, f32[1,128,8,64]{1,3,2,0:T(8,128)}, u32[]{:S(2)}) copy-start(f32[1,128,8,64]{1,3,2,0:T(8,128)} %get-tuple-element.660) | copy-start | bytes 786436
  666.3 66.6 %copy-start.12 = (f32[1,128,512]{1,2,0:T(8,128)S(1)}, f32[1,128,512]{1,2,0:T(8,128)}, u32[]{:S(2)}) copy-start(f32[1,128,512]{1,2,0:T(8,128)} %get-tuple-element.957) | copy-start | bytes 786436
  666.3 66.6 %copy-start.22 = (f32[1,1,512]{1,2,0:T(8,128)S(1)}, f32[1,1,512]{1,2,0:T(8,128)}, u32[]{:S(2)}) copy-start(f32[1,1,512]{1,2,0:T(8,128)} %copy.220) | copy-start | bytes 6148
  732.2 5.2 copy-start.1
  (23 other events, 41.6 us)
Sparse Core Ops, SparseCore 0:
  9.8 75.0 all-gather.7
  251.6 68.9 all-gather.5
  323.0 71.5 all-gather.9
  396.3 66.6 all-gather.11
  468.3 263.9 all-reduce.60
